TPU v7x, 32 devices: a whole 2x2x4 slice. The times are simulated.
32 devices in a mesh: dp: 8 (over z, x), tensor: 4 (over y, core).
Axes of the slice: x: 2, y: 2, z: 4, core: 2. Of those that a mesh axis runs over, the one named last changes fastest.
Arguments:
- tokens: bfloat16 [8192, 768], P(('dp', 'tensor')), may hold values from -6 to 6
- timestep: int32 [8], P('dp'), may hold values from 0 to 999
- block_size: int32 [8], P('dp'), may hold values from 128 to 512, as said below
- table: bfloat16 [1000, 768], replicated, may hold values from -6 to 6
- ln1_gain: bfloat16 [2, 768], replicated, may hold values from 0.5 to 1.5
- ln1_bias: bfloat16 [2, 768], replicated, may hold values from -3 to 3
- w_qkv: bfloat16 [2, 768, 3, 768], P(None, None, None, 'tensor'), may hold values from -0.21875 to 0.21875
- w_out: bfloat16 [2, 768, 768], P(None, 'tensor'), may hold values from -0.875 to 0.875
- b_out: bfloat16 [2, 768], replicated, may hold values from -3 to 3
- ln2_gain: bfloat16 [2, 768], replicated, may hold values from 0.5 to 1.5
- ln2_bias: bfloat16 [2, 768], replicated, may hold values from -3 to 3
- w_up: bfloat16 [2, 768, 3072], P(None, None, 'tensor'), may hold values from -0.21875 to 0.21875
- b_up: bfloat16 [2, 3072], P(None, 'tensor'), may hold values from -3 to 3
- w_down: bfloat16 [2, 3072, 768], P(None, 'tensor'), may hold values from -0.109375 to 0.109375
- b_down: bfloat16 [2, 768], replicated, may hold values from -3 to 3
- cotangent: bfloat16 [8192, 768], P(('dp', 'tensor')), may hold values from -6 to 6
Outputs:
- output: bfloat16 [8192, 768], P(('dp', 'tensor'))
- grad_tokens: float32 [8192, 768], P(('dp', 'tensor'))
- grad_table: float32 [1000, 768], P(None, 'dp')
- grad_ln1_gain: float32 [2, 768], P(None, 'dp')
- grad_ln1_bias: float32 [2, 768], P(None, 'dp')
- grad_w_qkv: float32 [2, 768, 3, 768], P(None, 'dp', None, 'tensor')
- grad_w_out: float32 [2, 768, 768], P(None, 'tensor', 'dp')
- grad_b_out: float32 [2, 768], P(None, 'dp')
- grad_ln2_gain: float32 [2, 768], P(None, 'dp')
- grad_ln2_bias: float32 [2, 768], P(None, 'dp')
- grad_w_up: float32 [2, 768, 3072], P(None, 'dp', 'tensor')
- grad_b_up: float32 [2, 3072], P(None, ('tensor', 'dp'))
- grad_w_down: float32 [2, 3072, 768], P(None, 'tensor', 'dp')
- grad_b_down: float32 [2, 768], P(None, 'dp')
Inputs may be any that keep to these rules, and one draw needn't show every extreme that they name: `block_size`: every sequence's block length is 128, 256 or 512, and all three occur.
All inputs are finite; a program needn't handle non-finite values.
Results may differ from a plain program's by a relative error of at most 0.019.
Values may be sent and summed in bfloat16 or wider, within the bound.
A program may use at most 192 MiB of HBM per device.

v0:
```python
import jax
import jax.numpy as jnp
from jax import lax
from jax.sharding import PartitionSpec as P

HEAD_DIM = 64


HIGH = lax.Precision.HIGHEST
EPSILON = 1e-05
NEGATIVE = -1e30


def norm_apply(hidden, gain, bias):
    mean = jnp.mean(hidden, axis=-1, keepdims=True)
    centred = hidden - mean
    spread = jnp.mean(centred * centred, axis=-1, keepdims=True)
    return centred * lax.rsqrt(spread + EPSILON) * gain + bias


def gelu_exact(values):
    return jax.nn.gelu(values, approximate=False)


def block_mask(length, block):
    where = jnp.arange(length, dtype=jnp.int32) // block
    return where[None, :] <= where[:, None]


def masked_scores(query, keys, block):
    scaling = HEAD_DIM ** (-0.5)
    scores = jnp.einsum("qhe,khe->hqk", query, keys, preferred_element_type=jnp.float32) * scaling
    return jnp.where(block_mask(query.shape[0], block)[None], scores, NEGATIVE)


def attend_forward(query, keys, values, block):
    scores = masked_scores(query, keys, block)
    top_score = jnp.max(scores, axis=-1, keepdims=True)
    expo = jnp.exp(scores - top_score)
    total = jnp.sum(expo, axis=-1, keepdims=True)
    weights = (expo / total).astype(jnp.bfloat16)
    mixed = jnp.einsum("hqk,khe->qhe", weights, values, preferred_element_type=jnp.float32)
    return (mixed.astype(jnp.bfloat16), (top_score + jnp.log(total))[..., 0])


def attend_back(query, keys, values, grad_mixed, log_total, block):
    scaling = HEAD_DIM ** (-0.5)
    scores = masked_scores(query, keys, block)
    prob = jnp.exp(scores - log_total[..., None])
    weights = prob.astype(jnp.bfloat16)
    grad_values = jnp.einsum(
        "hqk,qhe->khe", weights, grad_mixed, preferred_element_type=jnp.float32
    )
    grad_prob = jnp.einsum("qhe,khe->hqk", grad_mixed, values, preferred_element_type=jnp.float32)
    inner = jnp.sum(prob * grad_prob, axis=-1, keepdims=True)
    grad_scores = (prob * (grad_prob - inner)).astype(jnp.bfloat16)
    grad_query = (
        jnp.einsum("hqk,khe->qhe", grad_scores, keys, preferred_element_type=jnp.float32) * scaling
    )
    grad_keys = (
        jnp.einsum("hqk,qhe->khe", grad_scores, query, preferred_element_type=jnp.float32) * scaling
    )
    return jnp.stack([grad_query, grad_keys, grad_values], axis=1).astype(jnp.bfloat16)


def local(
    tokens,
    timestep,
    block_size,
    table,
    ln1_gain,
    ln1_bias,
    w_qkv,
    w_out,
    b_out,
    ln2_gain,
    ln2_bias,
    w_up,
    b_up,
    w_down,
    b_down,
    cotangent,
):
    row_count = tokens.shape[0]
    tensor_count = lax.axis_size("tensor")
    all_rows = row_count * tensor_count
    seq_count = timestep.shape[0]
    length = all_rows // seq_count
    layer_count = w_qkv.shape[0]
    local_heads = w_qkv.shape[-1] // HEAD_DIM
    step_total = table.shape[0]
    first_row = lax.axis_index("tensor") * row_count
    row_seq = (first_row + jnp.arange(row_count, dtype=jnp.int32)) // length
    seq_pick = (row_seq[:, None] == jnp.arange(seq_count, dtype=jnp.int32)[None, :]).astype(
        jnp.float32
    )
    step_pick = timestep[:, None] == jnp.arange(step_total, dtype=jnp.int32)[None, :]
    seq_embed = jnp.dot(step_pick.astype(jnp.bfloat16), table, preferred_element_type=jnp.float32)
    hidden = tokens.astype(jnp.float32) + jnp.dot(seq_pick, seq_embed, precision=HIGH)
    kept = []
    for layer_index in range(layer_count):
        gain_one = ln1_gain[layer_index].astype(jnp.float32)
        bias_one = ln1_bias[layer_index].astype(jnp.float32)
        gain_two = ln2_gain[layer_index].astype(jnp.float32)
        bias_two = ln2_bias[layer_index].astype(jnp.float32)
        normed = norm_apply(hidden, gain_one, bias_one).astype(jnp.bfloat16)
        full_normed = lax.all_gather(normed, "tensor", axis=0, tiled=True)
        projected = jnp.einsum(
            "td,dcf->tcf", full_normed, w_qkv[layer_index], preferred_element_type=jnp.float32
        ).astype(jnp.bfloat16)
        split = projected.reshape(seq_count, length, 3, local_heads, HEAD_DIM)
        mixed, log_total = lax.map(
            lambda entry: attend_forward(entry[0][:, 0], entry[0][:, 1], entry[0][:, 2], entry[1]),
            (split, block_size),
        )
        mixed_flat = mixed.reshape(all_rows, local_heads * HEAD_DIM)
        out_weight = w_out[layer_index]
        attended = lax.psum_scatter(
            jnp.dot(mixed_flat, out_weight, preferred_element_type=jnp.float32).astype(
                jnp.bfloat16
            ),
            "tensor",
            scatter_dimension=0,
            tiled=True,
        ).astype(jnp.float32) + b_out[layer_index].astype(jnp.float32)
        middle = hidden + attended
        normed_two = norm_apply(middle, gain_two, bias_two).astype(jnp.bfloat16)
        full_two = lax.all_gather(normed_two, "tensor", axis=0, tiled=True)
        pre_act = jnp.dot(full_two, w_up[layer_index], preferred_element_type=jnp.float32) + b_up[
            layer_index
        ].astype(jnp.float32)
        activated = gelu_exact(pre_act).astype(jnp.bfloat16)
        down_weight = w_down[layer_index]
        feed = lax.psum_scatter(
            jnp.dot(activated, down_weight, preferred_element_type=jnp.float32).astype(
                jnp.bfloat16
            ),
            "tensor",
            scatter_dimension=0,
            tiled=True,
        ).astype(jnp.float32) + b_down[layer_index].astype(jnp.float32)
        kept.append(
            (
                hidden,
                full_normed,
                projected,
                mixed_flat,
                log_total,
                middle,
                full_two,
                pre_act,
                activated,
            )
        )
        hidden = middle + feed
    output = hidden.astype(jnp.bfloat16)
    residual_grad = cotangent.astype(jnp.float32)
    collected = [None] * layer_count
    for layer_index in reversed(range(layer_count)):
        (
            hidden_in,
            full_normed,
            projected,
            mixed_flat,
            log_total,
            middle,
            full_two,
            pre_act,
            activated,
        ) = kept[layer_index]
        gain_one = ln1_gain[layer_index].astype(jnp.float32)
        bias_one = ln1_bias[layer_index].astype(jnp.float32)
        gain_two = ln2_gain[layer_index].astype(jnp.float32)
        bias_two = ln2_bias[layer_index].astype(jnp.float32)
        grad_feed = residual_grad.astype(jnp.bfloat16)
        full_grad_feed = lax.all_gather(grad_feed, "tensor", axis=0, tiled=True)
        grad_b_down = jnp.sum(grad_feed.astype(jnp.float32), axis=0)
        grad_w_down = jnp.einsum(
            "tf,td->fd", activated, full_grad_feed, preferred_element_type=jnp.float32
        )
        grad_act = jnp.einsum(
            "td,fd->tf", full_grad_feed, w_down[layer_index], preferred_element_type=jnp.float32
        )
        gelu_value, gelu_pull = jax.vjp(gelu_exact, pre_act)
        grad_pre = gelu_pull(grad_act)[0].astype(jnp.bfloat16)
        grad_b_up = jnp.sum(grad_pre.astype(jnp.float32), axis=0)
        grad_w_up = jnp.einsum("td,tf->df", full_two, grad_pre, preferred_element_type=jnp.float32)
        up_weight = w_up[layer_index]
        grad_normed_two = lax.psum_scatter(
            jnp.einsum("tf,df->td", grad_pre, up_weight, preferred_element_type=jnp.float32).astype(
                jnp.bfloat16
            ),
            "tensor",
            scatter_dimension=0,
            tiled=True,
        ).astype(jnp.float32)
        norm_value, norm_pull = jax.vjp(norm_apply, middle, gain_two, bias_two)
        grad_middle, grad_gain_two, grad_bias_two = norm_pull(grad_normed_two)
        grad_middle = grad_middle + residual_grad
        grad_attended = grad_middle.astype(jnp.bfloat16)
        full_grad_attended = lax.all_gather(grad_attended, "tensor", axis=0, tiled=True)
        grad_b_out = jnp.sum(grad_attended.astype(jnp.float32), axis=0)
        grad_w_out = jnp.einsum(
            "tc,td->cd", mixed_flat, full_grad_attended, preferred_element_type=jnp.float32
        )
        grad_mixed = jnp.einsum(
            "td,cd->tc", full_grad_attended, w_out[layer_index], preferred_element_type=jnp.float32
        ).astype(jnp.bfloat16)
        split = projected.reshape(seq_count, length, 3, local_heads, HEAD_DIM)
        grad_split = grad_mixed.reshape(seq_count, length, local_heads, HEAD_DIM)
        grad_projected = lax.map(
            lambda entry: attend_back(
                entry[0][:, 0], entry[0][:, 1], entry[0][:, 2], entry[1], entry[2], entry[3]
            ),
            (split, grad_split, log_total, block_size),
        )
        grad_projected = grad_projected.reshape(all_rows, 3, local_heads * HEAD_DIM)
        grad_w_qkv = jnp.einsum(
            "td,tcf->dcf", full_normed, grad_projected, preferred_element_type=jnp.float32
        )
        qkv_weight = w_qkv[layer_index]
        grad_normed = lax.psum_scatter(
            jnp.einsum(
                "tcf,dcf->td", grad_projected, qkv_weight, preferred_element_type=jnp.float32
            ).astype(jnp.bfloat16),
            "tensor",
            scatter_dimension=0,
            tiled=True,
        ).astype(jnp.float32)
        first_value, first_pull = jax.vjp(norm_apply, hidden_in, gain_one, bias_one)
        grad_hidden, grad_gain_one, grad_bias_one = first_pull(grad_normed)
        residual_grad = grad_hidden + grad_middle
        matrices = (grad_w_qkv, grad_w_out, grad_w_up, grad_b_up, grad_w_down)
        collected[layer_index] = (
            matrices,
            (grad_gain_one, grad_bias_one, grad_b_out, grad_gain_two, grad_bias_two, grad_b_down),
        )
    seq_sum = jnp.einsum("ts,td->sd", seq_pick, residual_grad, precision=HIGH)
    smalls = tuple(
        (
            jnp.stack([collected[index][1][member] for index in range(layer_count)])
            for member in range(6)
        )
    )
    summed = (
        lax.psum(seq_sum.astype(jnp.bfloat16), "tensor").astype(jnp.float32),
        lax.psum(smalls[0].astype(jnp.bfloat16), "tensor").astype(jnp.float32),
        lax.psum(smalls[1].astype(jnp.bfloat16), "tensor").astype(jnp.float32),
        lax.psum(smalls[2].astype(jnp.bfloat16), "tensor").astype(jnp.float32),
        lax.psum(smalls[3].astype(jnp.bfloat16), "tensor").astype(jnp.float32),
        lax.psum(smalls[4].astype(jnp.bfloat16), "tensor").astype(jnp.float32),
        lax.psum(smalls[5].astype(jnp.bfloat16), "tensor").astype(jnp.float32),
    )
    stacked = tuple(
        (
            jnp.stack([collected[index][0][member] for index in range(layer_count)])
            for member in range(5)
        )
    )
    every_step = lax.all_gather(timestep, "dp", axis=0, tiled=True)
    columns = lax.all_to_all(summed[0], "dp", split_axis=1, concat_axis=0, tiled=True)
    every_pick = (every_step[:, None] == jnp.arange(step_total, dtype=jnp.int32)[None, :]).astype(
        jnp.float32
    )
    grad_table = jnp.einsum("sn,sd->nd", every_pick, columns, precision=HIGH)
    everything = (
        lax.psum_scatter(summed[1], "dp", scatter_dimension=1, tiled=True),
        lax.psum_scatter(summed[2], "dp", scatter_dimension=1, tiled=True),
        lax.psum_scatter(summed[3], "dp", scatter_dimension=1, tiled=True),
        lax.psum_scatter(summed[4], "dp", scatter_dimension=1, tiled=True),
        lax.psum_scatter(summed[5], "dp", scatter_dimension=1, tiled=True),
        lax.psum_scatter(summed[6], "dp", scatter_dimension=1, tiled=True),
        lax.psum_scatter(stacked[0], "dp", scatter_dimension=1, tiled=True),
        lax.psum_scatter(stacked[1], "dp", scatter_dimension=2, tiled=True),
        lax.psum_scatter(stacked[2], "dp", scatter_dimension=1, tiled=True),
        lax.psum_scatter(stacked[3], "dp", scatter_dimension=1, tiled=True),
        lax.psum_scatter(stacked[4], "dp", scatter_dimension=2, tiled=True),
    )
    small_done = everything[:6]
    matrix_done = everything[6:]
    return (
        output,
        residual_grad,
        grad_table,
        small_done[0],
        small_done[1],
        matrix_done[0],
        matrix_done[1],
        small_done[2],
        small_done[3],
        small_done[4],
        matrix_done[2],
        matrix_done[3],
        matrix_done[4],
        small_done[5],
    )


def solution(mesh):
    placed = (
        P(("dp", "tensor"), None),
        P("dp"),
        P("dp"),
        P(),
        P(),
        P(),
        P(None, None, None, "tensor"),
        P(None, "tensor", None),
        P(),
        P(),
        P(),
        P(None, None, "tensor"),
        P(None, "tensor"),
        P(None, "tensor", None),
        P(),
        P(("dp", "tensor"), None),
    )
    return jax.shard_map(
        local,
        mesh=mesh,
        in_specs=placed,
        out_specs=(
            P(("dp", "tensor"), None),
            P(("dp", "tensor"), None),
            P(None, "dp"),
            P(None, "dp"),
            P(None, "dp"),
            P(None, "dp", None, "tensor"),
            P(None, "tensor", "dp"),
            P(None, "dp"),
            P(None, "dp"),
            P(None, "dp"),
            P(None, "dp", "tensor"),
            P(None, ("tensor", "dp")),
            P(None, "tensor", "dp"),
            P(None, "dp"),
        ),
        check_vma=False,
    )
```

profile of v0, /device:TPU:0, one launch (start us, length us, event | category | flops | bytes accessed | tf_op | source)
XLA Modules:
  0.0 1440.7 jit_solution(17351174674459709161)
XLA Ops:
  18.5 19.0 %all-gather.9.cloned.1.call-done = bf16[1024,768]{1,0:T(8,128)(2,1)} async-done(((bf16[256,768]{1,0:T(8,128)(2,1)}), bf16[1024,768]{1,0:T(8,128)(2,1)}) %all-gather.9.cloned.1.call-update) | async-done | bytes 1572880 | tf_op jit(solution)/shard_map/all_gather | solution.py:107
  53.8 28.0 %reduce-scatter.37.cloned.1.call-done = bf16[256,768]{1,0:T(8,128)(2,1)} async-done(((bf16[1024,768]{1,0:T(8,128)(2,1)}), bf16[256,768]{1,0:T(8,128)(2,1)}) %reduce-scatter.37.cloned.1.call-update) | async-done | bytes 393232 | tf_op jit(solution)/shard_map/reduce_scatter | solution.py:118
  87.3 19.2 %all-gather.11.cloned.1.call-done = bf16[1024,768]{1,0:T(8,128)(2,1)} async-done(((bf16[256,768]{1,0:T(8,128)(2,1)}), bf16[1024,768]{1,0:T(8,128)(2,1)}) %all-gather.11.cloned.1.call-update) | async-done | bytes 1572880 | tf_op jit(solution)/shard_map/all_gather | solution.py:128
  106.4 11.6 multiply_convert_fusion.3
  121.8 28.0 %reduce-scatter.39.cloned.1.call-done = bf16[256,768]{1,0:T(8,128)(2,1)} async-done(((bf16[1024,768]{1,0:T(8,128)(2,1)}), bf16[256,768]{1,0:T(8,128)(2,1)}) %reduce-scatter.39.cloned.1.call-update) | async-done | bytes 393232 | tf_op jit(solution)/shard_map/reduce_scatter | solution.py:134
  152.7 19.6 %all-gather.13.cloned.1.call-done = bf16[1024,768]{1,0:T(8,128)(2,1)} async-done(((bf16[256,768]{1,0:T(8,128)(2,1)}), bf16[1024,768]{1,0:T(8,128)(2,1)}) %all-gather.13.cloned.1.call-update) | async-done | bytes 1572880 | tf_op jit(solution)/shard_map/all_gather | solution.py:107
  188.7 28.1 %reduce-scatter.41.cloned.1.call-done = bf16[256,768]{1,0:T(8,128)(2,1)} async-done(((bf16[1024,768]{1,0:T(8,128)(2,1)}), bf16[256,768]{1,0:T(8,128)(2,1)}) %reduce-scatter.41.cloned.1.call-update) | async-done | bytes 393232 | tf_op jit(solution)/shard_map/reduce_scatter | solution.py:118
  220.3 18.8 %all-gather.15.cloned.1.call-done = bf16[1024,768]{1,0:T(8,128)(2,1)} async-done(((bf16[256,768]{1,0:T(8,128)(2,1)}), bf16[1024,768]{1,0:T(8,128)(2,1)}) %all-gather.15.cloned.1.call-update) | async-done | bytes 1572880 | tf_op jit(solution)/shard_map/all_gather | solution.py:128
  239.0 11.8 multiply_convert_fusion.2
  250.8 9.4 all-gather.17.cloned.1.call-done
  274.4 23.8 %reduce-scatter.45.cloned.1.call-done = bf16[256,768]{1,0:T(8,128)(2,1)} async-done(((bf16[1024,768]{1,0:T(8,128)(2,1)}), bf16[256,768]{1,0:T(8,128)(2,1)}) %reduce-scatter.45.cloned.1.call-update) | async-done | bytes 393232 | tf_op jit(solution)/shard_map/reduce_scatter | solution.py:189
  299.6 29.0 %reduce-scatter.43.cloned.1.call-done = bf16[256,768]{1,0:T(8,128)(2,1)} async-done(((bf16[1024,768]{1,0:T(8,128)(2,1)}), bf16[256,768]{1,0:T(8,128)(2,1)}) %reduce-scatter.43.cloned.1.call-update) | async-done | bytes 393232 | tf_op jit(solution)/shard_map/reduce_scatter | solution.py:134
  333.1 19.3 %all-gather.19.cloned.1.call-done = bf16[1024,768]{1,0:T(8,128)(2,1)} async-done(((bf16[256,768]{1,0:T(8,128)(2,1)}), bf16[1024,768]{1,0:T(8,128)(2,1)}) %all-gather.19.cloned.1.call-update) | async-done | bytes 1572880 | tf_op jit(solution)/shard_map/all_gather | solution.py:201
  384.7 28.1 %reduce-scatter.47.cloned.1.call-done = bf16[256,768]{1,0:T(8,128)(2,1)} async-done(((bf16[1024,768]{1,0:T(8,128)(2,1)}), bf16[256,768]{1,0:T(8,128)(2,1)}) %reduce-scatter.47.cloned.1.call-update) | async-done | bytes 393232 | tf_op jit(solution)/shard_map/reduce_scatter | solution.py:222
  418.3 19.7 %all-gather.21.cloned.1.call-done = bf16[1024,768]{1,0:T(8,128)(2,1)} async-done(((bf16[256,768]{1,0:T(8,128)(2,1)}), bf16[1024,768]{1,0:T(8,128)(2,1)}) %all-gather.21.cloned.1.call-update) | async-done | bytes 1572880 | tf_op jit(solution)/shard_map/all_gather | solution.py:176
  447.8 28.1 %reduce-scatter.49.cloned.1.call-done = bf16[256,768]{1,0:T(8,128)(2,1)} async-done(((bf16[1024,768]{1,0:T(8,128)(2,1)}), bf16[256,768]{1,0:T(8,128)(2,1)}) %reduce-scatter.49.cloned.1.call-update) | async-done | bytes 393232 | tf_op jit(solution)/shard_map/reduce_scatter | solution.py:189
  480.2 19.5 %all-gather.23.cloned.1.call-done = bf16[1024,768]{1,0:T(8,128)(2,1)} async-done(((bf16[256,768]{1,0:T(8,128)(2,1)}), bf16[1024,768]{1,0:T(8,128)(2,1)}) %all-gather.23.cloned.1.call-update) | async-done | bytes 1572880 | tf_op jit(solution)/shard_map/all_gather | solution.py:201
  543.4 8.2 copy.60
  571.1 10.3 all-reduce.2
  602.7 6.9 copy.75
  609.6 8.0 reshape.361
  627.4 12.3 all-reduce
  645.7 151.2 %all-reduce.5.cloned.1.call-done = f32[2,768,768]{1,0,2:T(2,128)} async-done(((f32[2,768,768]{1,0,2:T(2,128)}), f32[2,768,768]{1,0,2:T(2,128)}) %all-reduce.5.cloned.1.call-update) | async-done | bytes 4718608
  798.9 65.2 %reduce-scatter.61.cloned.1.call-done = f32[96,384]{1,0:T(8,128)} async-done(((f32[768,384]{1,0:T(8,128)}), f32[96,384]{1,0:T(8,128)}) %reduce-scatter.61.cloned.1.call-update) | async-done | bytes 147472
  867.2 61.8 %reduce-scatter.55.cloned.1.call-done = f32[96,2]{1,0:T(8,128)} async-done(((f32[768,2]{1,0:T(8,128)}), f32[96,2]{1,0:T(8,128)}) %reduce-scatter.55.cloned.1.call-update) | async-done | bytes 784
  930.5 63.1 %reduce-scatter.57.cloned.1.call-done = f32[96,2]{1,0:T(8,128)} async-done(((f32[768,2]{1,0:T(8,128)}), f32[96,2]{1,0:T(8,128)}) %reduce-scatter.57.cloned.1.call-update) | async-done | bytes 784
  995.0 63.1 %reduce-scatter.63.cloned.1.call-done = f32[96,2]{1,0:T(8,128)} async-done(((f32[768,2]{1,0:T(8,128)}), f32[96,2]{1,0:T(8,128)}) %reduce-scatter.63.cloned.1.call-update) | async-done | bytes 784
  1059.6 63.2 %reduce-scatter.65.cloned.1.call-done = f32[96,2]{1,0:T(8,128)} async-done(((f32[768,2]{1,0:T(8,128)}), f32[96,2]{1,0:T(8,128)}) %reduce-scatter.65.cloned.1.call-update) | async-done | bytes 784
  1124.2 62.9 %reduce-scatter.67.cloned.1.call-done = f32[96,2]{1,0:T(8,128)} async-done(((f32[768,2]{1,0:T(8,128)}), f32[96,2]{1,0:T(8,128)}) %reduce-scatter.67.cloned.1.call-update) | async-done | bytes 784
  1188.5 63.2 %reduce-scatter.71.cloned.1.call-done = f32[96,2]{1,0:T(8,128)} async-done(((f32[768,2]{1,0:T(8,128)}), f32[96,2]{1,0:T(8,128)}) %reduce-scatter.71.cloned.1.call-update) | async-done | bytes 784
  1253.2 80.5 %reduce-scatter.59.cloned.1.call-done = f32[96,1152]{1,0:T(8,128)} async-done(((f32[768,1152]{1,0:T(8,128)}), f32[96,1152]{1,0:T(8,128)}) %reduce-scatter.59.cloned.1.call-update) | async-done | bytes 442384
  1336.2 97.2 %reduce-scatter.53.cloned.1.call-done = f32[2,96,768]{2,1,0:T(8,128)} async-done(((f32[2,768,768]{2,1,0:T(8,128)}), f32[2,96,768]{2,1,0:T(8,128)}) %reduce-scatter.53.cloned.1.call-update) | async-done | bytes 589840 | tf_op jit(solution)/shard_map/reduce_scatter | solution.py:275
  (343 shorter events, 244.4 us)
Async XLA Ops:
  7.2 30.2 %all-gather.9.cloned.1.call-start = ((), (), s32[]{:S(2)}) async-start(), calls=%async_computation.19 | async-start | bytes 1966080 | tf_op jit(solution)/shard_map/all_gather | solution.py:107
  14.9 66.9 %reduce-scatter.37.cloned.1.call-start = ((), (), s32[]{:S(2)}) async-start(), calls=%async_computation.20 | async-start | bytes 1966080 | tf_op jit(solution)/shard_map/reduce_scatter | solution.py:118
  51.8 35.4 %copy-start.45 = (bf16[2,768]{1,0:T(2,128)(2,1)S(1)}, bf16[2,768]{1,0:T(2,128)(2,1)}, u32[]{:S(2)}) copy-start(bf16[2,768]{1,0:T(2,128)(2,1)} %param.28) | copy-start | bytes 9220
  53.6 52.8 %all-gather.11.cloned.1.call-start = ((), (), s32[]{:S(2)}) async-start(), calls=%async_computation.21 | async-start | bytes 1966080 | tf_op jit(solution)/shard_map/all_gather | solution.py:128
  86.7 63.2 %reduce-scatter.39.cloned.1.call-start = ((), (), s32[]{:S(2)}) async-start(), calls=%async_computation.22 | async-start | bytes 1966080 | tf_op jit(solution)/shard_map/reduce_scatter | solution.py:134
  121.8 50.6 %all-gather.13.cloned.1.call-start = ((), (), s32[]{:S(2)}) async-start(), calls=%async_computation.23 | async-start | bytes 1966080 | tf_op jit(solution)/shard_map/all_gather | solution.py:107
  152.5 64.3 %reduce-scatter.41.cloned.1.call-start = ((), (), s32[]{:S(2)}) async-start(), calls=%async_computation.24 | async-start | bytes 1966080 | tf_op jit(solution)/shard_map/reduce_scatter | solution.py:118
  188.7 50.3 %all-gather.15.cloned.1.call-start = ((), (), s32[]{:S(2)}) async-start(), calls=%async_computation.25 | async-start | bytes 1966080 | tf_op jit(solution)/shard_map/all_gather | solution.py:128
  219.3 41.0 %all-gather.17.cloned.1.call-start = ((), (), s32[]{:S(2)}) async-start(), calls=%async_computation.27 | async-start | bytes 1966080 | tf_op jit(solution)/shard_map/all_gather | solution.py:176
  220.0 78.1 %reduce-scatter.45.cloned.1.call-start = ((), (), s32[]{:S(2)}) async-start(), calls=%async_computation.28 | async-start | bytes 1966080 | tf_op jit(solution)/shard_map/reduce_scatter | solution.py:189
  270.0 58.5 %reduce-scatter.43.cloned.1.call-start = ((), (), s32[]{:S(2)}) async-start(), calls=%async_computation.26 | async-start | bytes 1966080 | tf_op jit(solution)/shard_map/reduce_scatter | solution.py:134
  274.3 57.3 %copy-start.13 = (bf16[256,768]{1,0:T(8,128)(2,1)S(1)}, bf16[256,768]{1,0:T(8,128)(2,1)}, u32[]{:S(2)}) copy-start(bf16[256,768]{1,0:T(8,128)(2,1)} %param.31) | copy-start | bytes 1179652
  274.3 78.0 %all-gather.19.cloned.1.call-start = ((), (), s32[]{:S(2)}) async-start(), calls=%async_computation.29 | async-start | bytes 1966080 | tf_op jit(solution)/shard_map/all_gather | solution.py:201
  332.6 80.2 %reduce-scatter.47.cloned.1.call-start = ((), (), s32[]{:S(2)}) async-start(), calls=%async_computation.30 | async-start | bytes 1966080 | tf_op jit(solution)/shard_map/reduce_scatter | solution.py:222
  384.6 53.4 %all-gather.21.cloned.1.call-start = ((), (), s32[]{:S(2)}) async-start(), calls=%async_computation.31 | async-start | bytes 1966080 | tf_op jit(solution)/shard_map/all_gather | solution.py:176
  418.2 57.7 %reduce-scatter.49.cloned.1.call-start = ((), (), s32[]{:S(2)}) async-start(), calls=%async_computation.32 | async-start | bytes 1966080 | tf_op jit(solution)/shard_map/reduce_scatter | solution.py:189
  447.8 52.0 %copy-start.35 = (bf16[2,192,768]{2,1,0:T(8,128)(2,1)S(1)}, bf16[2,192,768]{2,1,0:T(8,128)(2,1)}, u32[]{:S(2)}) copy-start(bf16[2,192,768]{2,1,0:T(8,128)(2,1)} %param.23) | copy-start | bytes 1769476
  447.8 52.0 %all-gather.23.cloned.1.call-start = ((), (), s32[]{:S(2)}) async-start(), calls=%async_computation.33 | async-start | bytes 1966080 | tf_op jit(solution)/shard_map/all_gather | solution.py:201
  480.0 85.0 %reduce-scatter.51.cloned.1.call-start = ((), (), s32[]{:S(2)}) async-start(), calls=%async_computation.34 | async-start | bytes 1966080 | tf_op jit(solution)/shard_map/reduce_scatter | solution.py:222
  531.4 109.0 %reduce-scatter.69.cloned.1.call-start = ((), (), s32[]{:S(2)}) async-start(), calls=%async_computation.43 | async-start | bytes 442368
  537.2 259.8 %all-reduce.5.cloned.1.call-start = ((), (), s32[]{:S(2)}) async-start(), calls=%async_computation.45 | async-start | bytes 9437184
  551.7 312.5 %reduce-scatter.61.cloned.1.call-start = ((), (), s32[]{:S(2)}) async-start(), calls=%async_computation.39 | async-start | bytes 1327104
  564.5 364.6 %reduce-scatter.55.cloned.1.call-start = ((), (), s32[]{:S(2)}) async-start(), calls=%async_computation.36 | async-start | bytes 442368
  582.4 411.2 %reduce-scatter.57.cloned.1.call-start = ((), (), s32[]{:S(2)}) async-start(), calls=%async_computation.37 | async-start | bytes 442368
  583.4 474.8 %reduce-scatter.63.cloned.1.call-start = ((), (), s32[]{:S(2)}) async-start(), calls=%async_computation.40 | async-start | bytes 442368
  586.7 536.1 %reduce-scatter.65.cloned.1.call-start = ((), (), s32[]{:S(2)}) async-start(), calls=%async_computation.41 | async-start | bytes 442368
  590.6 596.5 %reduce-scatter.67.cloned.1.call-start = ((), (), s32[]{:S(2)}) async-start(), calls=%async_computation.42 | async-start | bytes 442368
  593.9 657.8 %reduce-scatter.71.cloned.1.call-start = ((), (), s32[]{:S(2)}) async-start(), calls=%async_computation.44 | async-start | bytes 442368
  599.0 734.7 %reduce-scatter.59.cloned.1.call-start = ((), (), s32[]{:S(2)}) async-start(), calls=%async_computation.38 | async-start | bytes 3981312
  617.7 815.8 %reduce-scatter.53.cloned.1.call-start = ((), (), s32[]{:S(2)}) async-start(), calls=%async_computation.35 | async-start | bytes 5308416 | tf_op jit(solution)/shard_map/reduce_scatter | solution.py:275
  642.4 223.7 %all-to-all-start = ((f32[1,8,96]{2,0,1:T(1,128)}), f32[1,8,96]{2,0,1:T(1,128)S(1)}, u32[]{:S(2)}, u32[]{:S(2)}) async-start(f32[1,8,96]{2,0,1:T(1,128)} %bitcast.43), calls=%async_computation.8 | async-start | bytes 8192 | tf_op jit(solution)/shard_map/all_to_all | solution.py:261
  645.7 787.7 %copy-start.1 = (bf16[1000,768]{1,0:T(8,128)(2,1)S(1)}, bf16[1000,768]{1,0:T(8,128)(2,1)}, u32[]{:S(2)}) copy-start(bf16[1000,768]{1,0:T(8,128)(2,1)} %param.19) | copy-start | bytes 4608004
  (60 other events, 443.9 us)
Sparse Core Ops, SparseCore 0:
  15.1 22.3 all-gather.8
  53.8 28.0 reduce-scatter.36
  86.8 19.6 all-gather.10
  121.9 27.9 reduce-scatter.38
  152.6 19.6 all-gather.12
  188.8 27.9 reduce-scatter.40
  219.4 19.6 all-gather.14
  240.6 19.6 all-gather.16
  270.1 27.9 reduce-scatter.44
  300.5 27.9 reduce-scatter.42
  332.7 19.5 all-gather.18
  384.8 27.9 reduce-scatter.46
  418.3 19.6 all-gather.20
  447.9 28.0 reduce-scatter.48
  480.1 19.6 all-gather.22
  531.5 27.9 reduce-scatter.50
  562.6 62.0 reduce-scatter.68
  628.2 168.6 all-reduce.4
  800.3 63.7 reduce-scatter.60
  867.8 61.1 reduce-scatter.54
  932.3 61.2 reduce-scatter.56
  996.9 61.2 reduce-scatter.62
  1061.4 61.2 reduce-scatter.64
  1125.9 61.2 reduce-scatter.66
  1190.4 61.3 reduce-scatter.70
  1255.2 78.4 reduce-scatter.58
  1337.7 95.6 reduce-scatter.52
where the time goes:
time: 1450 us; the launch traced here: 1440 us
  waiting for transfers between devices  1110 us (77%)
  matrix products  143 us (10%)
  local copies, waits for them, and re-layouts  74.7 us (5%)
  other arithmetic  66 us (5%)
  blocking collectives  22.6 us (2%)
  between operations  18.2 us (1%)
    unnamed x37, waiting for transfers between devices  675 us
    reduce_scatter x1, waiting for transfers between devices, local(): lax.psum_scatter(stacked[2], 'dp', scatter_dimension=1, tiled=True)  97.2 us
    unnamed x155, local copies, waits for them, and re-layouts  65.3 us
    reduce_scatter x2, waiting for transfers between devices, local(): lax.psum_scatter(jnp.dot(activated, down_weight, preferred_element_type=j...  57 us
    reduce_scatter x2, waiting for transfers between devices, local(): lax.psum_scatter(jnp.dot(mixed_flat, out_weight, preferred_element_type=j...  56.1 us
    reduce_scatter x2, waiting for transfers between devices, local(): lax.psum_scatter(jnp.einsum('tf,df->td', grad_pre, up_weight, preferred_e...  51.9 us
    all_gather x2, waiting for transfers between devices, local(): lax.all_gather(grad_attended, 'tensor', axis=0, tiled=True)  38.8 us
    all_gather x2, waiting for transfers between devices, local(): full_normed = lax.all_gather(normed, 'tensor', axis=0, tiled=True)  38.6 us
  transfers between devices with their start and end apart: 28, of which 25 were waited for; matrix products, arithmetic and copies ran while one was open for 8% of the time, Pallas kernels for 0%

commit v1 on v0

v1 whole, which is shorter than its diff:
```python
import functools

import jax
import jax.numpy as jnp
from jax import lax
from jax.experimental import pallas as pl
from jax.experimental.pallas import tpu as pltpu
from jax.sharding import PartitionSpec as P

HEAD_DIM = 64
EPSILON = 1e-05
NEGATIVE = -1e30
MESH = pl.DeviceIdType.MESH
BF = jnp.bfloat16
F32 = jnp.float32
INV_SQRT2 = 0.7071067811865476
INV_SQRT2PI = 0.3989422804014327

NN = (((1,), (0,)), ((), ()))
NT = (((1,), (1,)), ((), ()))
TN = (((0,), (0,)), ((), ()))


def mm(a, b, dims=NN):
    return lax.dot_general(a, b, dims, preferred_element_type=F32)


def step_kernel(dim, *refs):
    (
        bs_ref, tok_in, cot_in, emb_in, vec_in, bup_in,
        wqkv_h, wout_h, wup_h, wdown_h,
        out_o, gtok_o, small_o, bupg_o, g_o,
        wqkv, wout, wup, wdown, tokf, cotf,
        a_b, a2_b, g_b, gp_b, qkvT, kv_b, oT_b, lse_b, h_b, m_b,
        df_b, dz_b, du_b, dh_b, doT_b, dqT_b, dkv_acc,
        ysend, yrecv, csend, crecv, part, s_b, p_b, ds_b, gtmp, gstage,
        small, smallr, bupg, outst,
        wsem, tsem_s, tsem_r, ysem_s, ysem_r, casem_s, casem_r, cpsem_s, cpsem_r,
        lsem, osem, gsem, ssem,
    ) = refs
    D, FL, HL, HP, R, L = dim["D"], dim["FL"], dim["HL"], dim["HP"], dim["R"], dim["L"]
    T = 4 * R
    NH = HL // HEAD_DIM
    CH = 2 * R
    NB = D // 256
    FB = FL // 256
    t = lax.axis_index("tensor")
    y = lax.div(t, 2)
    c = lax.rem(t, 2)
    ypeer = lax.rem(t + 2, 4)
    cpeer = t + 1 - 2 * c

    def own(r):
        return pl.multiple_of(R * (2 * r + c), R)

    def oth(r):
        return pl.multiple_of(R * (2 * r + 1 - c), R)

    def remote(src, dst, ss, rs, peer):
        return pltpu.make_async_remote_copy(
            src_ref=src, dst_ref=dst, send_sem=ss, recv_sem=rs,
            device_id={"tensor": peer}, device_id_type=MESH)

    bar = pltpu.get_barrier_semaphore()
    pl.semaphore_signal(bar, inc=1, device_id={"tensor": ypeer}, device_id_type=MESH)
    pl.semaphore_signal(bar, inc=1, device_id={"tensor": cpeer}, device_id_type=MESH)

    wcopies = []
    for l in range(L):
        row = []
        for i, (src, dst) in enumerate(((wqkv_h, wqkv), (wout_h, wout), (wup_h, wup), (wdown_h, wdown))):
            cp = pltpu.make_async_copy(src.at[l], dst.at[l], wsem.at[l, i])
            cp.start()
            row.append(cp)
        wcopies.append(row)
    loc = [pltpu.make_async_copy(tok_in, tokf.at[y], lsem.at[0]),
           pltpu.make_async_copy(cot_in, cotf.at[y], lsem.at[1])]
    for cp in loc:
        cp.start()
    pl.semaphore_wait(bar, 2)
    tcp = [remote(tok_in, tokf.at[y], tsem_s.at[0], tsem_r.at[0], ypeer),
           remote(cot_in, cotf.at[y], tsem_s.at[1], tsem_r.at[1], ypeer)]
    for cp in tcp:
        cp.start()

    small[...] = jnp.zeros_like(small)
    bupg[...] = jnp.zeros_like(bupg)
    dqT_b[...] = jnp.zeros_like(dqT_b)
    oT_b[...] = jnp.zeros_like(oT_b)
    bs = bs_ref[0]

    yc = {}
    pending = {}

    def y_copy(par, r):
        return remote(ysend.at[par, r], yrecv.at[par, r], ysem_s.at[par, r], ysem_r.at[par, r], ypeer)

    def tile_copy(buf, r):
        return remote(buf.at[pl.ds(own(r), R), :], buf.at[pl.ds(own(r), R), :],
                      casem_s.at[r], casem_r.at[r], cpeer)

    def part_copy(r):
        return remote(csend.at[r], crecv.at[r], cpsem_s.at[r], cpsem_r.at[r], cpeer)

    BLK = 32

    def rowloop(fn, init=0):
        return lax.fori_loop(0, R // BLK, lambda i, cy: fn(pl.multiple_of(i * BLK, BLK), cy), init)

    def ln_stats(x):
        mean = jnp.sum(x, axis=-1, keepdims=True) * (1.0 / D)
        xc = x - mean
        var = jnp.sum(xc * xc, axis=-1, keepdims=True) * (1.0 / D)
        return xc, lax.rsqrt(var + EPSILON)

    def enter_fwd(l, r, src, gi, dst_h, dst_a):
        gain = vec_in[l, gi : gi + 1, :]
        bias = vec_in[l, gi + 1 : gi + 2, :]

        def blk(i, cy):
            x = src(i)
            dst_h[l, r, pl.ds(i, BLK), :] = x
            xc, rstd = ln_stats(x)
            dst_a[l, pl.ds(pl.multiple_of(own(r) + i, BLK), BLK), :] = (xc * rstd * gain + bias).astype(BF)
            return cy

        rowloop(blk)
        cp = tile_copy(dst_a.at[l], r)
        cp.start()
        return cp

    def ysum(par, r, i):
        return ysend[par, r, pl.ds(i, BLK), :].astype(F32) + yrecv[par, r, pl.ds(i, BLK), :].astype(F32)

    def wait_y(par, r):
        cp = y_copy(par, r)
        cp.wait_send()
        cp.wait_recv()

    def send_partner(r, fill):
        fill(csend.at[r])
        cp = part_copy(r)
        cp.start()
        return cp

    def combine(par, r, cp):
        cp.wait_recv()

        def blk(i, cy):
            v = part[pl.ds(i, BLK), :] + crecv[r, pl.ds(i, BLK), :].astype(F32)
            ysend[par, r, pl.ds(i, BLK), :] = v.astype(BF)
            return cy

        rowloop(blk)
        cp.wait_send()
        y_copy(par, r).start()

    def qkv_tile(l, q0):
        def one(cc, cy):
            o = pl.multiple_of(cc * HP, HP)
            v = mm(wqkv[l, pl.ds(o, HP), :], a_b[l, pl.ds(q0, R), :], NT).astype(BF)
            qkvT[l, pl.ds(o, HP), pl.ds(q0, R)] = v
            return cy

        q = mm(wqkv[l, 0:HP, :], a_b[l, pl.ds(q0, R), :], NT).astype(BF)
        qkvT[l, 0:HP, pl.ds(q0, R)] = q * jnp.asarray(HEAD_DIM ** -0.5, BF)
        for cc in (1, 2):
            v = mm(wqkv[l, cc * HP : cc * HP + HP, :], a_b[l, pl.ds(q0, R), :], NT)
            qkvT[l, cc * HP : cc * HP + HP, pl.ds(q0, R)] = v.astype(BF)
            kv_b[l, cc - 1, pl.ds(q0, R), :] = v.T.astype(BF)

    def hmask(h):
        rows = lax.broadcasted_iota(jnp.int32, (HP, R), 0)
        return (rows >= h * HEAD_DIM) & (rows < (h + 1) * HEAD_DIM)

    def visible(r, kb, q0):
        key = lax.broadcasted_iota(jnp.int32, (R, R), 0) + (CH * r + kb * R)
        qry = lax.broadcasted_iota(jnp.int32, (R, R), 1) + q0
        return key <= (qry | (bs - 1))

    def att_fwd_tile(l, r, q0):
        KB = 2 * (r + 1)

        def head(h, cy):
            qm = jnp.where(hmask(h), qkvT[l, 0:HP, pl.ds(q0, R)].astype(F32), 0.0).astype(BF)
            top = None
            for kb in range(KB):
                s = mm(kv_b[l, 0, kb * R : kb * R + R, :], qm)
                if kb >= 2 * r:
                    s = jnp.where(visible(r, kb - 2 * r, q0), s, NEGATIVE)
                s_b[kb * R : kb * R + R, :] = s
                mx = jnp.max(s, axis=0, keepdims=True)
                top = mx if top is None else jnp.maximum(top, mx)
            tot = None
            for kb in range(KB):
                e = jnp.exp(s_b[kb * R : kb * R + R, :] - top)
                p_b[kb * R : kb * R + R, :] = e.astype(BF)
                sm = jnp.sum(e, axis=0, keepdims=True)
                tot = sm if tot is None else tot + sm
            hr = pl.multiple_of(h * HEAD_DIM, HEAD_DIM)
            o = mm(qkvT[l, pl.ds(pl.multiple_of(2 * HP + hr, HEAD_DIM), HEAD_DIM), 0 : KB * R], p_b[0 : KB * R, :])
            oT_b[l, pl.ds(hr, HEAD_DIM), pl.ds(q0, R)] = (o * (1.0 / tot)).astype(BF)
            lse_b[l, pl.ds(h, 1), pl.ds(q0, R)] = top + jnp.log(tot)
            return cy

        lax.fori_loop(0, NH, head, 0)

    def nblocks(fn, n):
        for i in range(n):
            fn(i * 256)

    def out_tile(l, q0, dst):
        o = oT_b[l, :, pl.ds(q0, R)].astype(F32).T.astype(BF)

        def one(n):
            dst[:, n : n + 256] = mm(o, wout[l, :, n : n + 256]).astype(dst.dtype)

        nblocks(one, NB)

    def up_tile(l, q0):
        def one(n, cy):
            n = pl.multiple_of(n * 256, 256)
            u = mm(a2_b[l, pl.ds(q0, R), :], wup[l, :, pl.ds(n, 256)]) + bup_in[l, :, pl.ds(n, 256)]
            phi = 0.5 * (1.0 + lax.erf(u * INV_SQRT2))
            g_b[l, pl.ds(q0, R), pl.ds(n, 256)] = (u * phi).astype(BF)
            gp = phi + u * (jnp.exp(u * u * -0.5) * INV_SQRT2PI)
            gp_b[l, pl.ds(q0, R), pl.ds(n, 256)] = gp.astype(BF)
            return cy

        lax.fori_loop(0, FB, one, 0)

    def down_tile(l, q0, dst):
        def one(n):
            dst[:, n : n + 256] = mm(g_b[l, pl.ds(q0, R), :], wdown[l, :, n : n + 256]).astype(dst.dtype)

        nblocks(one, NB)

    def att_fwd(l, r, tile_cp):
        qkv_tile(l, own(r))
        tile_cp.wait_recv()
        qkv_tile(l, oth(r))
        att_fwd_tile(l, r, oth(r))
        cp = send_partner(r, lambda ref: out_tile(l, oth(r), ref))
        att_fwd_tile(l, r, own(r))
        out_tile(l, own(r), part)
        tile_cp.wait_send()
        combine(0, r, cp)

    def ffn_fwd(l, r, tile_cp):
        up_tile(l, own(r))
        tile_cp.wait_recv()
        up_tile(l, oth(r))
        cp = send_partner(r, lambda ref: down_tile(l, oth(r), ref))
        down_tile(l, own(r), part)
        tile_cp.wait_send()
        combine(1, r, cp)

    for l in range(L):
        for r in range(2):
            if l == 0:
                if r == 0:
                    for cp in (loc[0], wcopies[0][0]):
                        cp.wait()
                    tcp[0].wait()
                src = lambda i, r=r: tokf[r, pl.ds(i, BLK), :].astype(F32) + emb_in[...]
            else:
                wait_y(1, r)
                bd = vec_in[l - 1, 5:6, :]
                src = lambda i, r=r, l=l, bd=bd: m_b[l - 1, r, pl.ds(i, BLK), :] + (ysum(1, r, i) + bd)
            if r == 0 and l > 0:
                wcopies[l][0].wait()
            cp = enter_fwd(l, r, src, 0, h_b, a_b)
            if r == 0:
                wcopies[l][1].wait()
            att_fwd(l, r, cp)
        for r in range(2):
            wait_y(0, r)
            bo = vec_in[l, 2:3, :]
            src = lambda i, r=r, l=l, bo=bo: h_b[l, r, pl.ds(i, BLK), :] + (ysum(0, r, i) + bo)
            if r == 0:
                wcopies[l][2].wait()
                wcopies[l][3].wait()
            cp = enter_fwd(l, r, src, 3, m_b, a2_b)
            ffn_fwd(l, r, cp)

    def finish_output(r):
        wait_y(1, r)
        bd = vec_in[L - 1, 5:6, :]

        def blk(i, cy):
            v = m_b[L - 1, r, pl.ds(i, BLK), :] + (ysum(1, r, i) + bd)
            outst[r, pl.ds(i, BLK), :] = v.astype(BF)
            return cy

        rowloop(blk)

    def ln_bwd(l, r, par, gi, xbuf, emit):
        gain = vec_in[l, gi : gi + 1, :]

        def blk(i, cy):
            dg, db = cy
            x = xbuf[l, r, pl.ds(i, BLK), :]
            dy = ysum(par, r, i)
            xc, rstd = ln_stats(x)
            xh = xc * rstd
            t1 = dy * gain
            m1 = jnp.sum(t1, axis=-1, keepdims=True) * (1.0 / D)
            m2 = jnp.sum(t1 * xh, axis=-1, keepdims=True) * (1.0 / D)
            dx = rstd * (t1 - m1 - xh * m2)
            emit(i, dx)
            dg = dg + jnp.sum(dy * xh, axis=0, keepdims=True)
            db = db + jnp.sum(dy, axis=0, keepdims=True)
            return (dg, db)

        z = jnp.zeros((1, D), F32)
        dg, db = rowloop(blk, (z, z))
        small[l, gi : gi + 1, :] = small[l, gi : gi + 1, :] + dg
        small[l, gi + 1 : gi + 2, :] = small[l, gi + 1 : gi + 2, :] + db

    def colsum_own(buf, r, l, row):
        def blk(i, cy):
            return cy + jnp.sum(buf[pl.ds(pl.multiple_of(own(r) + i, BLK), BLK), :].astype(F32), axis=0, keepdims=True)

        v = rowloop(blk, jnp.zeros((1, D), F32))
        small[l, row : row + 1, :] = small[l, row : row + 1, :] + v

    def enter_b1(l, r):
        if l == L - 1:
            def blk(i, cy):
                v = cotf[r, pl.ds(i, BLK), :]
                dh_b[r, pl.ds(i, BLK), :] = v.astype(F32)
                df_b[pl.ds(pl.multiple_of(own(r) + i, BLK), BLK), :] = v
                return cy

            rowloop(blk)
        else:
            wait_y(1, r)

            def emit(i, dx):
                v = dh_b[r, pl.ds(i, BLK), :] + dx
                dh_b[r, pl.ds(i, BLK), :] = v
                df_b[pl.ds(pl.multiple_of(own(r) + i, BLK), BLK), :] = v.astype(BF)

            ln_bwd(l + 1, r, 1, 0, h_b, emit)
        cp = tile_copy(df_b, r)
        cp.start()
        colsum_own(df_b, r, l, 5)
        return cp

    def du_tile(l, q0):
        def one(n, cy):
            n = pl.multiple_of(n * 256, 256)
            dg = mm(df_b[pl.ds(q0, R), :], wdown[l, pl.ds(n, 256), :], NT)
            du = (dg * gp_b[l, pl.ds(q0, R), pl.ds(n, 256)].astype(F32)).astype(BF)
            du_b[pl.ds(q0, R), pl.ds(n, 256)] = du
            bupg[l, :, pl.ds(n, 256)] = bupg[l, :, pl.ds(n, 256)] + jnp.sum(du.astype(F32), axis=0, keepdims=True)
            return cy

        lax.fori_loop(0, FB, one, 0)

    def da2_tile(l, q0, dst):
        def one(n):
            dst[:, n : n + 256] = mm(du_b[pl.ds(q0, R), :], wup[l, n : n + 256, :], NT).astype(dst.dtype)

        nblocks(one, NB)

    def ffn_bwd(l, r, tile_cp):
        du_tile(l, own(r))
        tile_cp.wait_recv()
        du_tile(l, oth(r))
        cp = send_partner(r, lambda ref: da2_tile(l, oth(r), ref))
        da2_tile(l, own(r), part)
        tile_cp.wait_send()
        combine(0, r, cp)

    def enter_b2(l, r):
        wait_y(0, r)

        def emit(i, dx):
            v = dh_b[r, pl.ds(i, BLK), :] + dx
            dh_b[r, pl.ds(i, BLK), :] = v
            dz_b[pl.ds(pl.multiple_of(own(r) + i, BLK), BLK), :] = v.astype(BF)

        ln_bwd(l, r, 0, 3, m_b, emit)
        cp = tile_copy(dz_b, r)
        cp.start()
        colsum_own(dz_b, r, l, 2)
        return cp

    def do_tile(l, q0):
        doT_b[:, pl.ds(q0, R)] = mm(wout[l], dz_b[pl.ds(q0, R), :], NT).astype(BF)

    def att_bwd_tile(l, r, q0):
        KB = 2 * (r + 1)
        KN = KB * R

        def head(h, cy):
            hr = pl.multiple_of(h * HEAD_DIM, HEAD_DIM)
            hm = hmask(h)
            qm = jnp.where(hm, qkvT[l, 0:HP, pl.ds(q0, R)].astype(F32), 0.0).astype(BF)
            dom = jnp.where(hm, doT_b[:, pl.ds(q0, R)].astype(F32), 0.0).astype(BF)
            do_h = doT_b[pl.ds(hr, HEAD_DIM), pl.ds(q0, R)]
            q_h = qkvT[l, pl.ds(hr, HEAD_DIM), pl.ds(q0, R)]
            o_h = oT_b[l, pl.ds(hr, HEAD_DIM), pl.ds(q0, R)]
            dsum = jnp.sum(do_h.astype(F32) * o_h.astype(F32), axis=0, keepdims=True)
            lse = lse_b[l, pl.ds(h, 1), pl.ds(q0, R)]
            for kb in range(KB):
                ks = slice(kb * R, kb * R + R)
                s = mm(kv_b[l, 0, ks, :], qm)
                p = jnp.exp(s - lse)
                if kb >= 2 * r:
                    p = jnp.where(visible(r, kb - 2 * r, q0), p, 0.0)
                p_b[ks, :] = p.astype(BF)
                dp = mm(kv_b[l, 1, ks, :], dom)
                ds_b[ks, :] = (p * (dp - dsum)).astype(BF)
            dkv_acc[1, pl.ds(hr, HEAD_DIM), 0:KN] = dkv_acc[1, pl.ds(hr, HEAD_DIM), 0:KN] + mm(do_h, p_b[0:KN, :], NT)
            dkv_acc[0, pl.ds(hr, HEAD_DIM), 0:KN] = dkv_acc[0, pl.ds(hr, HEAD_DIM), 0:KN] + mm(q_h, ds_b[0:KN, :], NT)
            k_h = qkvT[l, pl.ds(pl.multiple_of(HP + hr, HEAD_DIM), HEAD_DIM), 0:KN]
            dq = mm(k_h, ds_b[0:KN, :]) * (HEAD_DIM ** -0.5)
            dqT_b[pl.ds(hr, HEAD_DIM), pl.ds(q0, R)] = dq.astype(BF)
            return cy

        lax.fori_loop(0, NH, head, 0)

    def da_tile(l, q0, dst):
        dqkv = dqT_b[:, pl.ds(q0, R)].astype(F32).T.astype(BF)

        def one(n):
            dst[:, n : n + 256] = mm(dqkv, wqkv[l, :, n : n + 256]).astype(dst.dtype)

        nblocks(one, NB)

    def att_bwd(l, r, tile_cp):
        do_tile(l, own(r))
        att_bwd_tile(l, r, own(r))
        tile_cp.wait_recv()
        do_tile(l, oth(r))
        att_bwd_tile(l, r, oth(r))
        cs = slice(CH * r, CH * r + CH)
        for j in range(2):
            dqT_b[HP * (j + 1) : HP * (j + 1) + HL, cs] = dkv_acc[j, 0:HL, cs].astype(BF)
        cp = send_partner(r, lambda ref: da_tile(l, oth(r), ref))
        da_tile(l, own(r), part)
        tile_cp.wait_send()
        combine(1, r, cp)

    gcount = [0]

    def g_out(l, j):
        cp = pltpu.make_async_copy(gstage, g_o.at[l, j], gsem)
        cp.start()
        cp.wait()

    def wgrad_ffn(l):
        for j, (lhs, rhs) in ((1, (a2_b.at[l], du_b)), (2, (df_b, g_b.at[l]))):
            for n in range(NB):
                lt = lhs[:, n * 256 : n * 256 + 256].astype(F32).T.astype(BF)
                for f in range(FB):
                    gstage[n * 256 : n * 256 + 256, f * 256 : f * 256 + 256] = mm(lt, rhs[:, f * 256 : f * 256 + 256])
            g_out(l, j)

    def wgrad_att(l):
        for n in range(NB):
            ns = slice(n * 256, n * 256 + 256)
            for j in range(3):
                gtmp[j * HL : j * HL + HL, :] = mm(dqT_b[j * HP : j * HP + HL, :], a_b[l, :, ns])
            gtmp[3 * HL : 4 * HL, :] = mm(oT_b[l, 0:HL, :], dz_b[:, ns])
            gstage[ns, 0 : 4 * HL] = gtmp[...].T
        g_out(l, 0)

    loc[1].wait()
    tcp[1].wait()
    for l in range(L - 1, -1, -1):
        for r in (1, 0):
            cp = enter_b1(l, r)
            if l == L - 1:
                finish_output(r)
            ffn_bwd(l, r, cp)
        wgrad_ffn(l)
        dkv_acc[...] = jnp.zeros_like(dkv_acc)
        for r in (1, 0):
            cp = enter_b2(l, r)
            att_bwd(l, r, cp)
        wgrad_att(l)
    ocp = pltpu.make_async_copy(outst.at[y], out_o, osem.at[0])
    ocp.start()
    for r in (1, 0):
        wait_y(1, r)

        def emit(i, dx, r=r):
            dh_b[r, pl.ds(i, BLK), :] = dh_b[r, pl.ds(i, BLK), :] + dx

        ln_bwd(0, r, 1, 0, h_b, emit)

        def blk(i, cy, r=r):
            return cy + jnp.sum(dh_b[r, pl.ds(i, BLK), :], axis=0, keepdims=True)

        v = rowloop(blk, jnp.zeros((1, D), F32))
        small[0, 6:7, :] = small[0, 6:7, :] + v
    gcp = pltpu.make_async_copy(dh_b.at[y], gtok_o, osem.at[1])
    gcp.start()
    scp = remote(small, smallr, ssem.at[0], ssem.at[1], cpeer)
    scp.start()
    scp.wait()
    small_o[...] = small[...] + smallr[...]
    bupg_o[...] = bupg[...]
    ocp.wait()
    gcp.wait()


def run_step(bs, tok, cot, emb, vec, bup, wqkv, wout, wup, wdown):
    R, D = tok.shape
    L, _, FL = wup.shape
    HP = wout.shape[1]
    HL = dims_hl(HP)
    T = 4 * R
    dim = dict(D=D, FL=FL, HL=HL, HP=HP, R=R, L=L)
    vm = pl.BlockSpec(memory_space=pltpu.VMEM)
    any_ = pl.BlockSpec(memory_space=pl.ANY)
    dma = pltpu.SemaphoreType.DMA
    V = pltpu.VMEM
    return pl.pallas_call(
        functools.partial(step_kernel, dim),
        out_shape=(
            jax.ShapeDtypeStruct((R, D), BF),
            jax.ShapeDtypeStruct((R, D), F32),
            jax.ShapeDtypeStruct((L, 8, D), F32),
            jax.ShapeDtypeStruct((L, 1, FL), F32),
            jax.ShapeDtypeStruct((L, 3, D, FL), F32),
        ),
        in_specs=[pl.BlockSpec(memory_space=pltpu.SMEM), vm, vm, vm, vm, vm] + [any_] * 4,
        out_specs=(any_, any_, vm, vm, any_),
        scratch_shapes=[
            V((L, 3 * HP, D), BF), V((L, HP, D), BF), V((L, D, FL), BF), V((L, FL, D), BF),
            V((2, R, D), BF), V((2, R, D), BF),
            V((L, T, D), BF), V((L, T, D), BF), V((L, T, FL), BF), V((L, T, FL), BF),
            V((L, 3 * HP, T), BF), V((L, 2, T, HP), BF), V((L, HP, T), BF), V((L, 8, T), F32),
            V((L, 2, R, D), F32), V((L, 2, R, D), F32),
            V((T, D), BF), V((T, D), BF), V((T, FL), BF), V((2, R, D), F32),
            V((HP, T), BF), V((3 * HP, T), BF), V((2, HP, T), F32),
            V((2, 2, R, D), BF), V((2, 2, R, D), BF), V((2, R, D), BF), V((2, R, D), BF),
            V((R, D), F32), V((T, R), F32), V((T, R), BF), V((T, R), BF), V((4 * HL, 256), F32), V((D, FL), F32),
            V((L, 8, D), F32), V((L, 8, D), F32), V((L, 1, FL), F32), V((2, R, D), BF),
            dma((L, 4)), dma((2,)), dma((2,)), dma((2, 2)), dma((2, 2)),
            dma((2,)), dma((2,)), dma((2,)), dma((2,)),
            dma((2,)), dma((2,)), dma, dma((2,)),
        ],
        compiler_params=pltpu.CompilerParams(
            collective_id=0, has_side_effects=True, vmem_limit_bytes=67043328),
        name="layers",
    )(bs, tok, cot, emb, vec, bup, wqkv, wout, wup, wdown)


def dims_hl(hp):
    return hp - HEAD_DIM


def local(tokens, timestep, block_size, table, ln1_gain, ln1_bias, w_qkv, w_out, b_out,
          ln2_gain, ln2_bias, w_up, b_up, w_down, b_down, cotangent):
    L, D, _, HL = w_qkv.shape
    FL = w_up.shape[-1]
    R = tokens.shape[0]
    dp = lax.axis_size("dp")
    pad = HEAD_DIM
    emb = lax.dynamic_slice_in_dim(table, timestep[0], 1, 0).astype(F32)
    zero = jnp.zeros_like(b_out)
    vec = jnp.stack([ln1_gain, ln1_bias, b_out, ln2_gain, ln2_bias, b_down, zero, zero], axis=1).astype(F32)
    bup = b_up[:, None, :].astype(F32)
    wq = jnp.pad(jnp.transpose(w_qkv, (0, 2, 3, 1)), ((0, 0), (0, 0), (0, pad), (0, 0))).reshape(L, 3 * (HL + pad), D)
    wo = jnp.pad(w_out, ((0, 0), (0, pad), (0, 0)))
    out, gtok, small, bupg, g = run_step(block_size, tokens, cotangent, emb, vec, bup, wq, wo, w_up, w_down)
    per = D // dp
    gs = lax.psum_scatter(g, "dp", scatter_dimension=2, tiled=True)
    ssum = lax.psum_scatter(jnp.concatenate([small[:, :6], bupg], axis=1), "dp", scatter_dimension=2, tiled=True)
    cols = lax.all_to_all(small[0, 6:7], "dp", split_axis=1, concat_axis=0, tiled=True)
    steps = lax.all_gather(timestep, "dp", axis=0, tiled=True)
    pick = (steps[:, None] == jnp.arange(table.shape[0], dtype=jnp.int32)[None, :]).astype(F32)
    grad_table = jnp.einsum("sn,sd->nd", pick, cols, precision=lax.Precision.HIGHEST)
    gq = gs[:, 0, :, : 3 * HL].reshape(L, per, 3, HL)
    go = jnp.transpose(gs[:, 0, :, 3 * HL :], (0, 2, 1))
    gd = jnp.transpose(gs[:, 2], (0, 2, 1))
    return (out, gtok, grad_table, ssum[:, 0], ssum[:, 1], gq, go, ssum[:, 2], ssum[:, 3], ssum[:, 4],
            gs[:, 1], ssum[:, 6], gd, ssum[:, 5])


def solution(mesh):
    placed = (
        P(("dp", "tensor"), None), P("dp"), P("dp"), P(), P(), P(),
        P(None, None, None, "tensor"), P(None, "tensor", None), P(), P(), P(),
        P(None, None, "tensor"), P(None, "tensor"), P(None, "tensor", None), P(),
        P(("dp", "tensor"), None),
    )
    return jax.shard_map(
        local,
        mesh=mesh,
        in_specs=placed,
        out_specs=(
            P(("dp", "tensor"), None), P(("dp", "tensor"), None), P(None, "dp"), P(None, "dp"), P(None, "dp"),
            P(None, "dp", None, "tensor"), P(None, "tensor", "dp"), P(None, "dp"), P(None, "dp"), P(None, "dp"),
            P(None, "dp", "tensor"), P(None, ("tensor", "dp")), P(None, "tensor", "dp"), P(None, "dp"),
        ),
        check_vma=False,
    )
```

time: 1450 us -> 529 us (0.36)
  waiting for transfers between devices: 1110 us -> 268 us
  Pallas kernels: 0 us -> 187 us
  matrix products: 143 us -> 1.16 us
  other arithmetic: 66 us -> 2.75 us
  local copies, waits for them, and re-layouts: 74.7 us -> 28.1 us
    unnamed x37 -> x3, waiting for transfers between devices: 675 us -> 41.5 us
    pallas_call x0 -> x1, Pallas kernels: none -> 187 us  [run_step(): pl.pallas_call(functools.partial(step_kernel, dim), out_shape=(jax.ShapeD...]
    all_gather x8 -> x0, waiting for transfers between devices: 145 us -> none  [the longest x2 38.8 us: local(): lax.all_gather(grad_attended, 'tensor', axis=0, tiled=True)]
    dot_general x35 -> x1, matrix products: 130 us -> 1.16 us  [local(): jnp.einsum('sn,sd->nd', pick, cols, precision=lax.Precision.HIGHEST)]
    reduce_scatter x9 -> x1, waiting for transfers between devices: 290 us -> 226 us  [local(): gs = lax.psum_scatter(g, 'dp', scatter_dimension=2, tiled=True)]
    unnamed x155 -> x25, local copies, waits for them, and re-layouts: 65.3 us -> 12 us
    reduce_sum x24 -> x0, other arithmetic: 30 us -> none  [the longest x9 9.87 us: norm_apply(): return centred * lax.rsqrt(spread + EPSILON) * gain + bias]
    convert_element_type x8 -> x2, other arithmetic: 16.8 us -> 1.92 us  [the longest x1 1.29 us: local(): emb = lax.dynamic_slice_in_dim(table, timestep[0], 1, 0).astype(F32)]
  transfers between devices with their start and end apart: 28 -> 3, of which waited for: 25 -> 2; matrix products, arithmetic and copies ran while one was open for 8% -> 2% of each run, Pallas kernels for 0% -> 0%
where the time goes in v1:
time: 529 us; the launch traced here: 520 us
  waiting for transfers between devices  268 us (51%)
  Pallas kernels  187 us (35%)
  local copies, waits for them, and re-layouts  28.1 us (5%)
  between operations  15.9 us (3%)
  blocking collectives  11.9 us (2%)
  starting transfers between devices  5.88 us (1%)
    reduce_scatter x1, waiting for transfers between devices, local(): gs = lax.psum_scatter(g, 'dp', scatter_dimension=2, tiled=True)  226 us
    pallas_call x1, Pallas kernels, run_step(): pl.pallas_call(functools.partial(step_kernel, dim), out_shape=(jax.ShapeD...  187 us
    unnamed x3, waiting for transfers between devices  41.5 us
    unnamed x25, local copies, waits for them, and re-layouts  12 us
    unnamed x1, blocking collectives  11.9 us
  transfers between devices with their start and end apart: 3, of which 2 were waited for; matrix products, arithmetic and copies ran while one was open for 2% of the time, Pallas kernels for 0%

profile of v1, /device:TPU:0, one launch (start us, length us, event | category | flops | bytes accessed | tf_op | source)
XLA Modules:
  0.0 520.1 jit_solution(1926170798487554776)
XLA Ops:
  8.5 0.7 copy.41
  9.2 0.7 copy.42
  9.9 0.7 copy.43
  10.6 0.7 copy.44
  11.3 0.7 copy.45
  12.0 1.3 reshape.42.refs_5_
  13.2 0.7 copy.46
  14.7 2.0 pad.9.refs_7_
  16.6 3.0 pad.8
  19.7 1.3 dynamic-slice_convert_fusion.refs_3_
  21.0 187.0 %layers.1 = (bf16[256,768]{1,0:T(8,128)(2,1)}, f32[256,768]{1,0:T(8,128)}, f32[2,8,768]{2,1,0:T(8,128)}, f32[2,1,768]{2,1,0:T(1,128)}, f32[2,3,768,768]{3,2,1,0:T(8,128)}) custom-call(s32[1]{0:T(128)S(6)} %copy.64.refs_0_, bf16[256,768]{1,0:T(8,128)(2,1)} %refs_1_.1, bf16[256,768]{1,0:T(8,128)(2,1)} %refs_2_.1, f32[1,768]{1,0:T(1,128)} %dynamic-slice_convert_fusion.refs_3_, ...), custom_call_target="tpu_custom_call" | custom-call | tf_op jit(solution)/shard_map/layers/pallas_call | solution.py:522
  208.0 0.8 pad_maximum_fusion
  209.3 1.2 reshape.48
  210.6 0.7 reduce-scatter.5.cloned.1.call-update
  211.3 0.8 slice_reduce_fusion
  212.0 0.7 all_to_all.12
  212.7 5.8 %all-to-all-start = ((f32[1,8,96]{2,0,1:T(1,128)}), f32[1,8,96]{2,0,1:T(1,128)S(1)}, u32[]{:S(2)}, u32[]{:S(2)}) async-start(f32[1,8,96]{2,0,1:T(1,128)} %bitcast.10), calls=%async_computation | async-start | bytes 8192 | tf_op jit(solution)/shard_map/all_to_all | solution.py:575
  219.1 0.8 dynamic-update-slice
  219.8 11.9 %all-reduce.2 = s32[8]{0:T(128)S(1)} all-reduce(s32[8]{0:T(128)S(1)} %dynamic-update-slice), channel_id=1, replica_groups=mesh['dp'=8,'tensor'=4] {'dp'}, use_global_device_ids=true, to_apply=%add.2 | all-reduce | flops 8 | bytes 64
  231.7 1.2 fusion
  232.9 40.8 %reduce-scatter.7.cloned.1.call-done = f32[96,14]{1,0:T(8,128)} async-done(((f32[768,14]{1,0:T(8,128)}), f32[96,14]{1,0:T(8,128)}) %reduce-scatter.7.cloned.1.call-update) | async-done | bytes 5392
  273.7 0.9 reshape.49
  274.6 0.7 fusion.2
  275.3 0.7 copy.59
  279.8 226.0 %reduce-scatter.5.cloned.1.call-done = f32[2,3,96,768]{3,2,1,0:T(8,128)} async-done(((f32[2,3,768,768]{3,2,1,0:T(8,128)}), f32[2,3,96,768]{3,2,1,0:T(8,128)}) %reduce-scatter.5.cloned.1.call-update) | async-done | bytes 1769488 | tf_op jit(solution)/shard_map/reduce_scatter | solution.py:573
  505.8 1.0 slice_bitcast_fusion.2
  506.9 0.8 copy.50
  507.7 1.1 slice.54
  509.0 1.1 copy.49
  510.1 1.1 slice_bitcast_fusion
  511.2 0.7 copy.65
  511.9 0.9 copy.66
  (25 shorter events, 6.0 us)
Async XLA Ops:
  7.2 266.5 %reduce-scatter.7.cloned.1.call-start = ((), (), s32[]{:S(2)}) async-start(), calls=%async_computation.4 | async-start | bytes 442368
  210.5 295.3 %reduce-scatter.5.cloned.1.call-start = ((), (), s32[]{:S(2)}) async-start(), calls=%async_computation.3 | async-start | bytes 15925248 | tf_op jit(solution)/shard_map/reduce_scatter | solution.py:573
  210.6 7.9 %copy-start.3 = (u32[32]{0:T(128)S(1)}, u32[32]{0:T(128)}, u32[]{:S(2)}) copy-start(u32[32]{0:T(128)} %constant.15) | copy-start | bytes 388
  212.7 19.0 %all-to-all-start = ((f32[1,8,96]{2,0,1:T(1,128)}), f32[1,8,96]{2,0,1:T(1,128)S(1)}, u32[]{:S(2)}, u32[]{:S(2)}) async-start(f32[1,8,96]{2,0,1:T(1,128)} %bitcast.10), calls=%async_computation | async-start | bytes 8192 | tf_op jit(solution)/shard_map/all_to_all | solution.py:575
  506.9 3.2 copy-start
  509.0 2.2 copy-start.2
  510.1 1.8 copy-start.1
Sparse Core Ops, SparseCore 0:
  210.6 63.0 reduce-scatter.6
  277.3 228.4 reduce-scatter.4
